TPU v7x, 256 devices: a whole 4x4x8 slice. The times are simulated.
256 devices in a mesh: ta: 8 (over z), ha: 4 (over x_hi, core), wa: 8 (over x_lo, y).
Axes of the slice: x: 4 (x_hi: 2, x_lo: 2; x = x_hi * 2 + x_lo), y: 4, z: 8, core: 2. Of those that a mesh axis runs over, the one named last changes fastest.
Arguments:
- features: bfloat16 [32, 64, 128, 256], P('ta', 'ha', 'wa'), may hold values from -6 to 6
- norm_gain: float32 [256], replicated, may hold values from 0.5 to 1.5
- conv_weight: bfloat16 [3, 3, 3, 256, 256], replicated, may hold values from -0.078125 to 0.078125
- cotangent: bfloat16 [32, 64, 128, 256], P('ta', 'ha', 'wa'), may hold values from -6 to 6
Outputs:
- decoded: bfloat16 [32, 64, 128, 256], P('ta', 'ha', 'wa')
- grad_features: bfloat16 [32, 64, 128, 256], P('ta', 'ha', 'wa')
- grad_weight: float32 [3, 3, 3, 256, 256], P(None, None, None, None, ('ha', 'wa'))
All inputs are finite; a program needn't handle non-finite values.
Results may differ from a plain program's by a relative error of at most 0.0032.
Values may be sent and summed in bfloat16 or wider, within the bound.
A program may use at most 128 MiB of HBM per device.

v0:
```python
import jax
import jax.numpy as jnp
from jax import lax
from jax.sharding import PartitionSpec as P

EPSILON = 1e-06


def from_behind(array, axis, by):
    length = lax.axis_size(axis)
    pairs = [(i, i + by) for i in range(length) if 0 <= i + by < length]
    return lax.ppermute(array, axis, pairs)


def with_halo(cells, sides, width):
    for axis, dim in sides:
        count = lax.axis_size(axis)
        ends = count - 1
        head = lax.slice_in_dim(cells, 0, width, axis=dim)
        tail = lax.slice_in_dim(cells, cells.shape[dim] - width, cells.shape[dim], axis=dim)
        cells = jnp.concatenate(
            [
                lax.ppermute(tail, axis, [(i, (i + 1) % count) for i in range(ends)]),
                cells,
                lax.ppermute(head, axis, [((i + 1) % count, i) for i in range(ends)]),
            ],
            axis=dim,
        )
    return cells


def activate(features, norm_gain):
    values = features.astype(jnp.float32)
    inverse = lax.rsqrt(jnp.mean(values * values, axis=-1, keepdims=True) + EPSILON)
    unit_rms = values * inverse
    normed = unit_rms * norm_gain
    activated = (normed * jax.nn.sigmoid(normed)).astype(jnp.bfloat16)
    return (values, inverse, unit_rms, normed, activated)


def norm_backward(grad_act, normed, unit_rms, inverse, norm_gain):
    logistic = jax.nn.sigmoid(normed)
    grad_normed = grad_act * logistic * (1.0 + normed * (1.0 - logistic))
    grad_unit = grad_normed * norm_gain
    return inverse * (grad_unit - unit_rms * jnp.mean(grad_unit * unit_rms, axis=-1, keepdims=True))


def body(features, norm_gain, conv_weight, cotangent):
    frames, height, width, channels = features.shape
    values, inverse, unit_rms, normed, activated = activate(features, norm_gain)
    earlier = from_behind(activated[frames - 2 :], "ta", 1)
    padded = with_halo(jnp.concatenate([earlier, activated], 0), (("ha", 1), ("wa", 2)), 1)
    later = from_behind(cotangent[:2], "ta", -1)
    grad_padded = with_halo(jnp.concatenate([cotangent, later], 0), (("ha", 1), ("wa", 2)), 1)
    flat_grad = cotangent.reshape(-1, channels)
    mixed = jnp.zeros((frames * height * width, channels), jnp.float32)
    grad_act = jnp.zeros((frames * height * width, channels), jnp.float32)
    windows = []
    for t_off in range(3):
        for h_off in range(3):
            for w_off in range(3):
                window = padded[
                    t_off : t_off + frames, h_off : h_off + height, w_off : w_off + width
                ].reshape(-1, channels)
                windows.append(window)
                mixed = mixed + jnp.dot(
                    window, conv_weight[t_off, h_off, w_off], preferred_element_type=jnp.float32
                )
                back = grad_padded[
                    2 - t_off : 2 - t_off + frames,
                    2 - h_off : 2 - h_off + height,
                    2 - w_off : 2 - w_off + width,
                ].reshape(-1, channels)
                grad_act = grad_act + lax.dot_general(
                    back,
                    conv_weight[t_off, h_off, w_off],
                    (((1,), (1,)), ((), ())),
                    preferred_element_type=jnp.float32,
                )
    owners = lax.axis_size("ha") * lax.axis_size("wa")
    owned = channels // owners
    weight_taps = jnp.stack(
        [
            lax.dot_general(
                window, flat_grad, (((0,), (0,)), ((), ())), preferred_element_type=jnp.float32
            )
            for window in windows
        ]
    )
    shared = lax.psum_scatter(weight_taps, ("ha", "wa"), scatter_dimension=2, tiled=True)
    summed = lax.psum(shared, "ta")
    voxels_all = (
        frames * height * width * lax.axis_size("ta") * lax.axis_size("ha") * lax.axis_size("wa")
    )
    grad_weight = summed.reshape(3, 3, 3, channels, owned) * float(voxels_all) ** (-0.5)
    decoded = (values + mixed.reshape(features.shape)).astype(jnp.bfloat16)
    grad_norm = norm_backward(
        grad_act.reshape(features.shape), normed, unit_rms, inverse, norm_gain
    )
    grad_features = (cotangent.astype(jnp.float32) + grad_norm).astype(jnp.bfloat16)
    return (decoded, grad_features, grad_weight)


def solution(mesh):
    placed = (P("ta", "ha", "wa", None), P(), P(), P("ta", "ha", "wa", None))
    return jax.shard_map(
        body,
        mesh=mesh,
        in_specs=placed,
        out_specs=(
            P("ta", "ha", "wa", None),
            P("ta", "ha", "wa", None),
            P(None, None, None, None, ("ha", "wa")),
        ),
        check_vma=False,
    )
```

profile of v0, /device:TPU:2, one launch (start us, length us, event | category | flops | bytes accessed | tf_op | source)
XLA Modules:
  0.0 364.5 jit_solution(647792730584632596)
XLA Ops:
  7.2 1.0 slice.400
  8.2 1.3 collective-permute-start.5
  9.5 1.1 constant_dynamic-update-slice_fusion.1
  10.6 1.3 fusion.49
  11.8 6.5 %collective-permute-done.5 = bf16[2,16,16,256]{3,2,1,0:T(8,128)(2,1)S(1)} collective-permute-done((bf16[2,16,16,256]{3,2,1,0:T(8,128)(2,1)S(1)}, bf16[2,16,16,256]{3,2,1,0:T(8,128)(2,1)S(1)}, u32[]{:S(2)}, u32[]{:S(2)}) %collective-permute-start.5) | collective-permute-done | bytes 262176 | tf_op jit(solution)/shard_map/ppermute | solution.py:12
  18.3 1.3 collective-permute-start.6
  19.6 1.3 collective-permute-start.7
  21.0 4.1 %collective-permute-done.7 = bf16[6,1,16,256]{3,2,1,0:T(8,128)(2,1)S(1)} collective-permute-done((bf16[6,1,16,256]{3,2,1,0:T(8,128)(2,1)S(1)}, bf16[6,1,16,256]{3,2,1,0:T(8,128)(2,1)S(1)}, u32[]{:S(2)}, u32[]{:S(2)}) %collective-permute-start.7) | collective-permute-done | bytes 49184 | tf_op jit(solution)/shard_map/ppermute | solution.py:25
  25.3 5.8 %collective-permute-start.8 = (bf16[6,18,1,256]{3,2,1,0:T(2,128)(2,1)S(1)}, bf16[6,18,1,256]{3,2,1,0:T(2,128)(2,1)S(1)}, u32[]{:S(2)}, u32[]{:S(2)}) collective-permute-start(bf16[6,18,1,256]{3,2,1,0:T(2,128)(2,1)S(1)} %get-tuple-element.47), channel_id=1, source_target_pairs={{1,0},{2,1},{3,2},{4,3},{5,4},{6,5},{7,6},{9,8},{10,9},{11,10},{12... | collective-permute-start | bytes 165896 | tf_op jit(solution)/shard_map/ppermute | solution.py:25
  31.1 1.9 collective-permute-start.9
  33.0 0.6 pad_maximum_fusion.4
  34.0 5.9 %collective-permute-done.9 = bf16[6,18,1,256]{3,2,1,0:T(2,128)(2,1)S(1)} collective-permute-done((bf16[6,18,1,256]{3,2,1,0:T(2,128)(2,1)S(1)}, bf16[6,18,1,256]{3,2,1,0:T(2,128)(2,1)S(1)}, u32[]{:S(2)}, u32[]{:S(2)}) %collective-permute-start.9) | collective-permute-done | bytes 55328 | tf_op jit(solution)/shard_map/ppermute | solution.py:23
  39.9 0.9 pad_maximum_fusion.1
  40.7 3.3 fusion.191
  51.5 0.4 copy-done.4
  53.2 0.3 copy-done.2
  53.5 0.7 fusion.44
  54.3 1.6 fusion.48
  55.9 3.8 %collective-permute-start = (bf16[2,16,16,256]{3,2,1,0:T(8,128)(2,1)S(1)}, bf16[2,16,16,256]{3,2,1,0:T(8,128)(2,1)S(1)}, u32[]{:S(2)}, u32[]{:S(2)}) collective-permute-start(bf16[2,16,16,256]{3,2,1,0:T(8,128)(2,1)S(1)} %slice.431), channel_id=1, source_target_pairs={{0,32},{32,64},{64,96},{96,128},{128,160},{160,192},{192,224},{1,3... | collective-permute-start | bytes 786440 | tf_op jit(solution)/shard_map/ppermute | solution.py:12
  59.7 4.7 %collective-permute-done = bf16[2,16,16,256]{3,2,1,0:T(8,128)(2,1)S(1)} collective-permute-done((bf16[2,16,16,256]{3,2,1,0:T(8,128)(2,1)S(1)}, bf16[2,16,16,256]{3,2,1,0:T(8,128)(2,1)S(1)}, u32[]{:S(2)}, u32[]{:S(2)}) %collective-permute-start) | collective-permute-done | bytes 262176 | tf_op jit(solution)/shard_map/ppermute | solution.py:12
  64.4 1.3 collective-permute-start.2
  65.7 4.6 %collective-permute-start.1 = (bf16[6,1,16,256]{3,2,1,0:T(8,128)(2,1)S(1)}, bf16[6,1,16,256]{3,2,1,0:T(8,128)(2,1)S(1)}, u32[]{:S(2)}, u32[]{:S(2)}) collective-permute-start(bf16[6,1,16,256]{3,2,1,0:T(8,128)(2,1)S(1)} %get-tuple-element.77), channel_id=1, source_target_pairs={{0,8},{8,16},{16,24},{1,9},{9,17},{17,25},{2,10},{10,18},{18,26},{... | collective-permute-start | bytes 147464 | tf_op jit(solution)/shard_map/ppermute | solution.py:23
  70.3 0.9 collective-permute-done.1
  71.4 1.9 collective-permute-start.4
  73.3 4.1 %collective-permute-start.3 = (bf16[6,18,1,256]{3,2,1,0:T(2,128)(2,1)S(1)}, bf16[6,18,1,256]{3,2,1,0:T(2,128)(2,1)S(1)}, u32[]{:S(2)}, u32[]{:S(2)}) collective-permute-start(bf16[6,18,1,256]{3,2,1,0:T(2,128)(2,1)S(1)} %get-tuple-element.52), channel_id=1, source_target_pairs={{0,1},{1,2},{2,3},{3,4},{4,5},{5,6},{6,7},{8,9},{9,10},{10,11},{11... | collective-permute-start | bytes 165896 | tf_op jit(solution)/shard_map/ppermute | solution.py:23
  77.4 0.6 collective-permute-done.4
  78.0 4.0 %collective-permute-done.3 = bf16[6,18,1,256]{3,2,1,0:T(2,128)(2,1)S(1)} collective-permute-done((bf16[6,18,1,256]{3,2,1,0:T(2,128)(2,1)S(1)}, bf16[6,18,1,256]{3,2,1,0:T(2,128)(2,1)S(1)}, u32[]{:S(2)}, u32[]{:S(2)}) %collective-permute-start.3) | collective-permute-done | bytes 55328 | tf_op jit(solution)/shard_map/ppermute | solution.py:23
  82.0 0.9 pad_maximum_fusion
  83.0 1.1 fusion.30
  84.1 1.1 fusion.36
  85.1 1.0 fusion.29
  86.2 1.0 fusion.28
  87.2 1.0 fusion.11
  88.3 1.0 fusion.27
  89.3 1.1 fusion.26
  90.3 1.1 fusion.35
  91.4 1.1 fusion.25
  92.5 1.0 fusion.24
  93.5 1.0 fusion.34
  94.5 1.0 fusion.23
  95.6 1.0 fusion.22
  96.6 1.0 fusion.10
  97.6 1.1 fusion.21
  98.7 1.0 fusion.20
  99.7 1.1 fusion.33
  100.8 1.1 fusion.19
  101.9 1.0 fusion.18
  102.9 1.1 fusion.32
  104.0 1.1 fusion.17
  105.0 1.0 fusion.16
  106.1 1.0 fusion.15
  107.1 1.1 fusion.14
  108.1 1.0 fusion.13
  109.2 1.1 fusion.31
  110.2 1.0 fusion.12
  111.3 10.3 %copy.10 = f32[27,256,256]{1,0,2:T(8,128)} copy(f32[27,256,256]{2,1,0:T(8,128)} %fusion.12) | data formatting | bytes 14155776 | tf_op jit(solution)/shard_map/stack | solution.py:82
  122.3 1.6 copy-done.1
  124.3 0.4 fusion.194
  125.1 0.9 fusion.193
  133.5 146.3 %reduce-scatter.2.cloned.1.call-done = f32[27,256,8]{1,0,2:T(8,128)} async-done(((f32[27,256,256]{1,0,2:T(8,128)}), f32[27,256,8]{1,0,2:T(8,128)}) %reduce-scatter.2.cloned.1.call-update) | async-done | bytes 221200 | tf_op jit(solution)/shard_map/reduce_scatter | solution.py:90
  279.8 1.8 copy.11
  281.6 1.0 fusion.50
  282.6 73.5 %all-reduce.2.cloned.1.call-done = f32[27,256,8]{1,2,0:T(8,128)} async-done(((f32[27,256,8]{1,2,0:T(8,128)}), f32[27,256,8]{1,2,0:T(8,128)}) %all-reduce.2.cloned.1.call-update) | async-done | bytes 221200 | tf_op jit(solution)/shard_map/psum | solution.py:91
  356.0 1.6 broadcast_multiply_fusion
  (82 shorter events, 18.2 us)
Async XLA Ops:
  7.2 272.6 %reduce-scatter.2.cloned.1.call-start = ((), (), s32[]{:S(2)}) async-start(), calls=%async_computation.1 | async-start | bytes 8650752 | tf_op jit(solution)/shard_map/reduce_scatter | solution.py:90
  8.2 10.1 %collective-permute-start.5 = (bf16[2,16,16,256]{3,2,1,0:T(8,128)(2,1)S(1)}, bf16[2,16,16,256]{3,2,1,0:T(8,128)(2,1)S(1)}, u32[]{:S(2)}, u32[]{:S(2)}) collective-permute-start(bf16[2,16,16,256]{3,2,1,0:T(8,128)(2,1)S(1)} %slice.400), channel_id=1, source_target_pairs={{32,0},{64,32},{96,64},{128,96},{160,128},{192,160},{224,192},{33,... | collective-permute-start | bytes 786440 | tf_op jit(solution)/shard_map/ppermute | solution.py:12
  18.3 2.6 collective-permute-start.6
  19.6 5.5 %collective-permute-start.7 = (bf16[6,1,16,256]{3,2,1,0:T(8,128)(2,1)S(1)}, bf16[6,1,16,256]{3,2,1,0:T(8,128)(2,1)S(1)}, u32[]{:S(2)}, u32[]{:S(2)}) collective-permute-start(bf16[6,1,16,256]{3,2,1,0:T(8,128)(2,1)S(1)} %get-tuple-element.71), channel_id=1, source_target_pairs={{8,0},{16,8},{24,16},{9,1},{17,9},{25,17},{10,2},{18,10},{26,18},{... | collective-permute-start | bytes 147464 | tf_op jit(solution)/shard_map/ppermute | solution.py:25
  21.0 12.7 %copy-start = (bf16[3,3,3,256,256]{4,3,2,1,0:T(8,128)(2,1)S(1)}, bf16[3,3,3,256,256]{4,3,2,1,0:T(8,128)(2,1)}, u32[]{:S(2)}) copy-start(bf16[3,3,3,256,256]{4,3,2,1,0:T(8,128)(2,1)} %param.6) | copy-start | bytes 10616836
  25.3 8.7 %collective-permute-start.8 = (bf16[6,18,1,256]{3,2,1,0:T(2,128)(2,1)S(1)}, bf16[6,18,1,256]{3,2,1,0:T(2,128)(2,1)S(1)}, u32[]{:S(2)}, u32[]{:S(2)}) collective-permute-start(bf16[6,18,1,256]{3,2,1,0:T(2,128)(2,1)S(1)} %get-tuple-element.47), channel_id=1, source_target_pairs={{1,0},{2,1},{3,2},{4,3},{5,4},{6,5},{7,6},{9,8},{10,9},{11,10},{12... | collective-permute-start | bytes 165896 | tf_op jit(solution)/shard_map/ppermute | solution.py:25
  31.1 8.8 %collective-permute-start.9 = (bf16[6,18,1,256]{3,2,1,0:T(2,128)(2,1)S(1)}, bf16[6,18,1,256]{3,2,1,0:T(2,128)(2,1)S(1)}, u32[]{:S(2)}, u32[]{:S(2)}) collective-permute-start(bf16[6,18,1,256]{3,2,1,0:T(2,128)(2,1)S(1)} %get-tuple-element.48), channel_id=1, source_target_pairs={{0,1},{1,2},{2,3},{3,4},{4,5},{5,6},{6,7},{8,9},{9,10},{10,11},{11... | collective-permute-start | bytes 165896 | tf_op jit(solution)/shard_map/ppermute | solution.py:23
  50.8 1.0 copy-start.4
  52.5 1.0 copy-start.2
  52.5 1.0 copy-start.5
  55.9 8.5 %collective-permute-start = (bf16[2,16,16,256]{3,2,1,0:T(8,128)(2,1)S(1)}, bf16[2,16,16,256]{3,2,1,0:T(8,128)(2,1)S(1)}, u32[]{:S(2)}, u32[]{:S(2)}) collective-permute-start(bf16[2,16,16,256]{3,2,1,0:T(8,128)(2,1)S(1)} %slice.431), channel_id=1, source_target_pairs={{0,32},{32,64},{64,96},{96,128},{128,160},{160,192},{192,224},{1,3... | collective-permute-start | bytes 786440 | tf_op jit(solution)/shard_map/ppermute | solution.py:12
  64.4 5.9 %collective-permute-start.2 = (bf16[6,1,16,256]{3,2,1,0:T(8,128)(2,1)S(1)}, bf16[6,1,16,256]{3,2,1,0:T(8,128)(2,1)S(1)}, u32[]{:S(2)}, u32[]{:S(2)}) collective-permute-start(bf16[6,1,16,256]{3,2,1,0:T(8,128)(2,1)S(1)} %get-tuple-element.76), channel_id=1, source_target_pairs={{8,0},{16,8},{24,16},{9,1},{17,9},{25,17},{10,2},{18,10},{26,18},{... | collective-permute-start | bytes 147464 | tf_op jit(solution)/shard_map/ppermute | solution.py:25
  65.7 5.4 %collective-permute-start.1 = (bf16[6,1,16,256]{3,2,1,0:T(8,128)(2,1)S(1)}, bf16[6,1,16,256]{3,2,1,0:T(8,128)(2,1)S(1)}, u32[]{:S(2)}, u32[]{:S(2)}) collective-permute-start(bf16[6,1,16,256]{3,2,1,0:T(8,128)(2,1)S(1)} %get-tuple-element.77), channel_id=1, source_target_pairs={{0,8},{8,16},{16,24},{1,9},{9,17},{17,25},{2,10},{10,18},{18,26},{... | collective-permute-start | bytes 147464 | tf_op jit(solution)/shard_map/ppermute | solution.py:23
  71.4 6.6 %collective-permute-start.4 = (bf16[6,18,1,256]{3,2,1,0:T(2,128)(2,1)S(1)}, bf16[6,18,1,256]{3,2,1,0:T(2,128)(2,1)S(1)}, u32[]{:S(2)}, u32[]{:S(2)}) collective-permute-start(bf16[6,18,1,256]{3,2,1,0:T(2,128)(2,1)S(1)} %get-tuple-element.51), channel_id=1, source_target_pairs={{1,0},{2,1},{3,2},{4,3},{5,4},{6,5},{7,6},{9,8},{10,9},{11,10},{12... | collective-permute-start | bytes 165896 | tf_op jit(solution)/shard_map/ppermute | solution.py:25
  73.3 8.8 %collective-permute-start.3 = (bf16[6,18,1,256]{3,2,1,0:T(2,128)(2,1)S(1)}, bf16[6,18,1,256]{3,2,1,0:T(2,128)(2,1)S(1)}, u32[]{:S(2)}, u32[]{:S(2)}) collective-permute-start(bf16[6,18,1,256]{3,2,1,0:T(2,128)(2,1)S(1)} %get-tuple-element.52), channel_id=1, source_target_pairs={{0,1},{1,2},{2,3},{3,4},{4,5},{5,6},{6,7},{8,9},{9,10},{10,11},{11... | collective-permute-start | bytes 165896 | tf_op jit(solution)/shard_map/ppermute | solution.py:23
  121.6 234.4 %all-reduce.2.cloned.1.call-start = ((), (), s32[]{:S(2)}) async-start(), calls=%async_computation.2 | async-start | bytes 442368 | tf_op jit(solution)/shard_map/psum | solution.py:91
  121.9 2.0 copy-start.1
  132.9 148.7 %copy-start.3 = (bf16[4,16,16,256]{3,2,1,0:T(8,128)(2,1)S(1)}, bf16[4,16,16,256]{3,2,1,0:T(8,128)(2,1)}, u32[]{:S(2)}) copy-start(bf16[4,16,16,256]{3,2,1,0:T(8,128)(2,1)} %param.4) | copy-start | bytes 1572868
Sparse Core Ops, SparseCore 0:
  121.7 158.0 reduce-scatter.1
  282.7 73.2 all-reduce.1
where the time goes:
time: 365 us; the launch traced here: 364 us
  waiting for transfers between devices  246 us (67%)
  matrix products  45.2 us (12%)
  starting transfers between devices  27.6 us (8%)
  local copies, waits for them, and re-layouts  21.4 us (6%)
  between operations  14.7 us (4%)
  other arithmetic  9.12 us (2%)
    reduce_scatter x1, waiting for transfers between devices, body(): lax.psum_scatter(weight_taps, ('ha', 'wa'), scatter_dimension=2, tiled=True)  146 us
    psum x1, waiting for transfers between devices, body(): summed = lax.psum(shared, 'ta')  73.5 us
    dot_general x27, matrix products, body(): lax.dot_general(window, flat_grad, (((0,), (0,)), ((), ())), preferred_el...  28.3 us
    ppermute x4, starting transfers between devices, with_halo(): lax.ppermute(tail, axis, [(i, (i + 1) % count) for i in range(ends)])  11.9 us
    ppermute x2, waiting for transfers between devices, from_behind(): return lax.ppermute(array, axis, pairs)  11.2 us
    ppermute x4, waiting for transfers between devices, with_halo(): lax.ppermute(tail, axis, [(i, (i + 1) % count) for i in range(ends)])  10.8 us
    another operation x1, local copies, waits for them, and re-layouts, body(): jnp.stack([lax.dot_general(window, flat_grad, (((0,), (0,)), ((), ())), p...  10.3 us
    ppermute x4, starting transfers between devices, with_halo(): lax.ppermute(head, axis, [((i + 1) % count, i) for i in range(ends)])  10.3 us
  transfers between devices with their start and end apart: 12, of which 9 were waited for; matrix products, arithmetic and copies ran while one was open for 4% of the time, Pallas kernels for 0%

commit v1 on v0

--- a/solution.py
+++ b/solution.py
@@ -88,7 +88,8 @@
         ]
     )
     shared = lax.psum_scatter(weight_taps, ("ha", "wa"), scatter_dimension=2, tiled=True)
-    summed = lax.psum(shared, "ta")
+    view_the_fields = lambda my_data: jnp.sum(lax.all_gather(my_data, "ta"), axis=0)
+    summed = view_the_fields(shared)
     voxels_all = (
         frames * height * width * lax.axis_size("ta") * lax.axis_size("ha") * lax.axis_size("wa")
     )

time: 365 us -> 340 us (0.932)
  waiting for transfers between devices: 246 us -> 201 us
  matrix products: 45.2 us -> 54.9 us
  local copies, waits for them, and re-layouts: 21.4 us -> 29.4 us
    psum x1 -> x0, waiting for transfers between devices: 73.5 us -> none  [body(): summed = lax.psum(shared, 'ta')]
    all_gather x0 -> x1, waiting for transfers between devices: none -> 27.7 us  [body(): lax.all_gather(my_data, 'ta')]
    dot_general x27, matrix products: 7.99 us -> 17.5 us  [body(): jnp.dot(window, conv_weight[t_off, h_off, w_off], preferred_element_type=...]
    unnamed x13 -> x27, local copies, waits for them, and re-layouts: 3.45 us -> 7.9 us
  transfers between devices with their start and end apart: 12 -> 12, of which waited for: 9 -> 9; matrix products, arithmetic and copies ran while one was open for 4% -> 8% of each run, Pallas kernels for 0% -> 0%
where the time goes in v1:
time: 340 us; the launch traced here: 339 us
  waiting for transfers between devices  201 us (59%)
  matrix products  54.9 us (16%)
  local copies, waits for them, and re-layouts  29.4 us (9%)
  starting transfers between devices  27.6 us (8%)
  between operations  14.8 us (4%)
  other arithmetic  11.8 us (3%)
    reduce_scatter x1, waiting for transfers between devices, body(): lax.psum_scatter(weight_taps, ('ha', 'wa'), scatter_dimension=2, tiled=True)  146 us
    dot_general x27, matrix products, body(): lax.dot_general(window, flat_grad, (((0,), (0,)), ((), ())), preferred_el...  28.4 us
    all_gather x1, waiting for transfers between devices, body(): lax.all_gather(my_data, 'ta')  27.7 us
    dot_general x27, matrix products, body(): jnp.dot(window, conv_weight[t_off, h_off, w_off], preferred_element_type=...  17.5 us
    ppermute x4, starting transfers between devices, with_halo(): lax.ppermute(tail, axis, [(i, (i + 1) % count) for i in range(ends)])  11.9 us
    ppermute x2, waiting for transfers between devices, from_behind(): return lax.ppermute(array, axis, pairs)  11.3 us
    ppermute x4, waiting for transfers between devices, with_halo(): lax.ppermute(tail, axis, [(i, (i + 1) % count) for i in range(ends)])  10.8 us
    ppermute x4, starting transfers between devices, with_halo(): lax.ppermute(head, axis, [((i + 1) % count, i) for i in range(ends)])  10.3 us
  transfers between devices with their start and end apart: 12, of which 9 were waited for; matrix products, arithmetic and copies ran while one was open for 8% of the time, Pallas kernels for 0%

profile of v1, /device:TPU:2, one launch (start us, length us, event | category | flops | bytes accessed | tf_op | source)
XLA Modules:
  0.0 339.0 jit_solution(9465956731847675547)
XLA Ops:
  8.2 1.3 collective-permute-start.5
  9.5 1.1 constant_dynamic-update-slice_fusion.1
  10.6 1.3 fusion.49
  11.8 6.5 %collective-permute-done.5 = bf16[2,16,16,256]{3,2,1,0:T(8,128)(2,1)S(1)} collective-permute-done((bf16[2,16,16,256]{3,2,1,0:T(8,128)(2,1)S(1)}, bf16[2,16,16,256]{3,2,1,0:T(8,128)(2,1)S(1)}, u32[]{:S(2)}, u32[]{:S(2)}) %collective-permute-start.5) | collective-permute-done | bytes 262176 | tf_op jit(solution)/shard_map/ppermute | solution.py:12
  18.3 1.3 collective-permute-start.6
  19.6 1.3 collective-permute-start.7
  21.0 4.1 %collective-permute-done.7 = bf16[6,1,16,256]{3,2,1,0:T(8,128)(2,1)S(1)} collective-permute-done((bf16[6,1,16,256]{3,2,1,0:T(8,128)(2,1)S(1)}, bf16[6,1,16,256]{3,2,1,0:T(8,128)(2,1)S(1)}, u32[]{:S(2)}, u32[]{:S(2)}) %collective-permute-start.7) | collective-permute-done | bytes 49184 | tf_op jit(solution)/shard_map/ppermute | solution.py:25
  25.3 5.8 %collective-permute-start.8 = (bf16[6,18,1,256]{3,2,1,0:T(2,128)(2,1)S(1)}, bf16[6,18,1,256]{3,2,1,0:T(2,128)(2,1)S(1)}, u32[]{:S(2)}, u32[]{:S(2)}) collective-permute-start(bf16[6,18,1,256]{3,2,1,0:T(2,128)(2,1)S(1)} %get-tuple-element.44), channel_id=1, source_target_pairs={{1,0},{2,1},{3,2},{4,3},{5,4},{6,5},{7,6},{9,8},{10,9},{11,10},{12... | collective-permute-start | bytes 165896 | tf_op jit(solution)/shard_map/ppermute | solution.py:25
  31.1 1.9 collective-permute-start.9
  34.0 5.9 %collective-permute-done.9 = bf16[6,18,1,256]{3,2,1,0:T(2,128)(2,1)S(1)} collective-permute-done((bf16[6,18,1,256]{3,2,1,0:T(2,128)(2,1)S(1)}, bf16[6,18,1,256]{3,2,1,0:T(2,128)(2,1)S(1)}, u32[]{:S(2)}, u32[]{:S(2)}) %collective-permute-start.9) | collective-permute-done | bytes 55328 | tf_op jit(solution)/shard_map/ppermute | solution.py:23
  40.7 3.3 fusion.191
  54.3 1.6 fusion.48
  55.9 3.8 %collective-permute-start = (bf16[2,16,16,256]{3,2,1,0:T(8,128)(2,1)S(1)}, bf16[2,16,16,256]{3,2,1,0:T(8,128)(2,1)S(1)}, u32[]{:S(2)}, u32[]{:S(2)}) collective-permute-start(bf16[2,16,16,256]{3,2,1,0:T(8,128)(2,1)S(1)} %slice.431), channel_id=1, source_target_pairs={{0,32},{32,64},{64,96},{96,128},{128,160},{160,192},{192,224},{1,3... | collective-permute-start | bytes 786440 | tf_op jit(solution)/shard_map/ppermute | solution.py:12
  59.7 4.8 %collective-permute-done = bf16[2,16,16,256]{3,2,1,0:T(8,128)(2,1)S(1)} collective-permute-done((bf16[2,16,16,256]{3,2,1,0:T(8,128)(2,1)S(1)}, bf16[2,16,16,256]{3,2,1,0:T(8,128)(2,1)S(1)}, u32[]{:S(2)}, u32[]{:S(2)}) %collective-permute-start) | collective-permute-done | bytes 262176 | tf_op jit(solution)/shard_map/ppermute | solution.py:12
  64.5 1.3 collective-permute-start.2
  65.8 4.5 %collective-permute-start.1 = (bf16[6,1,16,256]{3,2,1,0:T(8,128)(2,1)S(1)}, bf16[6,1,16,256]{3,2,1,0:T(8,128)(2,1)S(1)}, u32[]{:S(2)}, u32[]{:S(2)}) collective-permute-start(bf16[6,1,16,256]{3,2,1,0:T(8,128)(2,1)S(1)} %get-tuple-element.74), channel_id=1, source_target_pairs={{0,8},{8,16},{16,24},{1,9},{9,17},{17,25},{2,10},{10,18},{18,26},{... | collective-permute-start | bytes 147464 | tf_op jit(solution)/shard_map/ppermute | solution.py:23
  71.4 1.9 collective-permute-start.4
  73.3 4.1 %collective-permute-start.3 = (bf16[6,18,1,256]{3,2,1,0:T(2,128)(2,1)S(1)}, bf16[6,18,1,256]{3,2,1,0:T(2,128)(2,1)S(1)}, u32[]{:S(2)}, u32[]{:S(2)}) collective-permute-start(bf16[6,18,1,256]{3,2,1,0:T(2,128)(2,1)S(1)} %get-tuple-element.49), channel_id=1, source_target_pairs={{0,1},{1,2},{2,3},{3,4},{4,5},{5,6},{6,7},{8,9},{9,10},{10,11},{11... | collective-permute-start | bytes 165896 | tf_op jit(solution)/shard_map/ppermute | solution.py:23
  78.0 4.0 %collective-permute-done.3 = bf16[6,18,1,256]{3,2,1,0:T(2,128)(2,1)S(1)} collective-permute-done((bf16[6,18,1,256]{3,2,1,0:T(2,128)(2,1)S(1)}, bf16[6,18,1,256]{3,2,1,0:T(2,128)(2,1)S(1)}, u32[]{:S(2)}, u32[]{:S(2)}) %collective-permute-start.3) | collective-permute-done | bytes 55328 | tf_op jit(solution)/shard_map/ppermute | solution.py:23
  83.0 1.1 fusion.30
  84.1 1.1 fusion.36
  85.2 1.0 fusion.29
  86.2 1.1 fusion.28
  87.3 1.1 fusion.11
  88.3 1.1 fusion.27
  89.4 1.1 fusion.26
  90.4 1.1 fusion.35
  91.5 1.1 fusion.25
  93.6 1.0 fusion.34
  94.6 1.0 fusion.23
  95.7 1.0 fusion.22
  96.7 1.1 fusion.10
  97.8 1.1 fusion.21
  98.8 1.1 fusion.20
  99.9 1.1 fusion.33
  101.0 1.0 fusion.19
  102.0 1.0 fusion.18
  105.1 1.1 fusion.16
  106.2 1.0 fusion.15
  107.2 1.1 fusion.14
  108.3 1.1 fusion.13
  109.3 1.0 fusion.31
  110.4 1.1 fusion.12
  111.4 10.3 %copy.7 = f32[27,256,256]{1,0,2:T(8,128)} copy(f32[27,256,256]{2,1,0:T(8,128)} %fusion.12) | data formatting | bytes 14155776 | tf_op jit(solution)/shard_map/stack | solution.py:82
  123.2 1.0 copy-done.1
  125.5 1.4 fusion.194
  127.2 1.8 fusion.193
  133.6 146.0 %reduce-scatter.2.cloned.1.call-done = f32[27,256,8]{1,0,2:T(8,128)} async-done(((f32[27,256,256]{1,0,2:T(8,128)}), f32[27,256,8]{1,0,2:T(8,128)}) %reduce-scatter.2.cloned.1.call-update) | async-done | bytes 221200 | tf_op jit(solution)/shard_map/reduce_scatter | solution.py:90
  279.5 1.8 copy.8
  281.4 1.4 convolution_add_fusion.31
  282.8 1.3 convolution_add_fusion.30
  284.1 1.2 convolution_add_fusion.29
  285.3 1.2 convolution_add_fusion.28
  286.5 1.3 convolution_add_fusion.27
  287.8 1.3 convolution_add_fusion.26
  289.1 1.2 convolution_add_fusion.25
  290.3 1.3 convolution_add_fusion.24
  291.6 1.2 convolution_add_fusion.23
  292.8 1.2 convolution_add_fusion.22
  295.0 27.7 %all-gather.3.cloned.1.call-done = f32[216,256,8]{1,2,0:T(8,128)} async-done(((f32[27,256,8]{1,2,0:T(8,128)}), f32[216,256,8]{1,2,0:T(8,128)}) %all-gather.3.cloned.1.call-update) | async-done | bytes 1769488 | tf_op jit(solution)/shard_map/all_gather | solution.py:91
  322.7 2.3 reduce_sum.29
  325.0 2.0 copy.38
  327.0 2.0 broadcast_multiply_fusion
  329.0 3.2 copy.10
  (97 shorter events, 27.2 us)
Async XLA Ops:
  7.2 272.4 %reduce-scatter.2.cloned.1.call-start = ((), (), s32[]{:S(2)}) async-start(), calls=%async_computation.1 | async-start | bytes 8650752 | tf_op jit(solution)/shard_map/reduce_scatter | solution.py:90
  8.2 10.1 %collective-permute-start.5 = (bf16[2,16,16,256]{3,2,1,0:T(8,128)(2,1)S(1)}, bf16[2,16,16,256]{3,2,1,0:T(8,128)(2,1)S(1)}, u32[]{:S(2)}, u32[]{:S(2)}) collective-permute-start(bf16[2,16,16,256]{3,2,1,0:T(8,128)(2,1)S(1)} %slice.400), channel_id=1, source_target_pairs={{32,0},{64,32},{96,64},{128,96},{160,128},{192,160},{224,192},{33,... | collective-permute-start | bytes 786440 | tf_op jit(solution)/shard_map/ppermute | solution.py:12
  18.3 2.6 collective-permute-start.6
  19.6 5.5 %collective-permute-start.7 = (bf16[6,1,16,256]{3,2,1,0:T(8,128)(2,1)S(1)}, bf16[6,1,16,256]{3,2,1,0:T(8,128)(2,1)S(1)}, u32[]{:S(2)}, u32[]{:S(2)}) collective-permute-start(bf16[6,1,16,256]{3,2,1,0:T(8,128)(2,1)S(1)} %get-tuple-element.68), channel_id=1, source_target_pairs={{8,0},{16,8},{24,16},{9,1},{17,9},{25,17},{10,2},{18,10},{26,18},{... | collective-permute-start | bytes 147464 | tf_op jit(solution)/shard_map/ppermute | solution.py:25
  21.0 12.7 %copy-start = (bf16[3,3,3,256,256]{4,3,2,1,0:T(8,128)(2,1)S(1)}, bf16[3,3,3,256,256]{4,3,2,1,0:T(8,128)(2,1)}, u32[]{:S(2)}) copy-start(bf16[3,3,3,256,256]{4,3,2,1,0:T(8,128)(2,1)} %param.6) | copy-start | bytes 10616836
  25.3 8.7 %collective-permute-start.8 = (bf16[6,18,1,256]{3,2,1,0:T(2,128)(2,1)S(1)}, bf16[6,18,1,256]{3,2,1,0:T(2,128)(2,1)S(1)}, u32[]{:S(2)}, u32[]{:S(2)}) collective-permute-start(bf16[6,18,1,256]{3,2,1,0:T(2,128)(2,1)S(1)} %get-tuple-element.44), channel_id=1, source_target_pairs={{1,0},{2,1},{3,2},{4,3},{5,4},{6,5},{7,6},{9,8},{10,9},{11,10},{12... | collective-permute-start | bytes 165896 | tf_op jit(solution)/shard_map/ppermute | solution.py:25
  31.1 8.8 %collective-permute-start.9 = (bf16[6,18,1,256]{3,2,1,0:T(2,128)(2,1)S(1)}, bf16[6,18,1,256]{3,2,1,0:T(2,128)(2,1)S(1)}, u32[]{:S(2)}, u32[]{:S(2)}) collective-permute-start(bf16[6,18,1,256]{3,2,1,0:T(2,128)(2,1)S(1)} %get-tuple-element.45), channel_id=1, source_target_pairs={{0,1},{1,2},{2,3},{3,4},{4,5},{5,6},{6,7},{8,9},{9,10},{10,11},{11... | collective-permute-start | bytes 165896 | tf_op jit(solution)/shard_map/ppermute | solution.py:23
  50.8 1.0 copy-start.4
  52.5 1.0 copy-start.2
  52.5 1.0 copy-start.11
  55.9 8.6 %collective-permute-start = (bf16[2,16,16,256]{3,2,1,0:T(8,128)(2,1)S(1)}, bf16[2,16,16,256]{3,2,1,0:T(8,128)(2,1)S(1)}, u32[]{:S(2)}, u32[]{:S(2)}) collective-permute-start(bf16[2,16,16,256]{3,2,1,0:T(8,128)(2,1)S(1)} %slice.431), channel_id=1, source_target_pairs={{0,32},{32,64},{64,96},{96,128},{128,160},{160,192},{192,224},{1,3... | collective-permute-start | bytes 786440 | tf_op jit(solution)/shard_map/ppermute | solution.py:12
  64.5 5.9 %collective-permute-start.2 = (bf16[6,1,16,256]{3,2,1,0:T(8,128)(2,1)S(1)}, bf16[6,1,16,256]{3,2,1,0:T(8,128)(2,1)S(1)}, u32[]{:S(2)}, u32[]{:S(2)}) collective-permute-start(bf16[6,1,16,256]{3,2,1,0:T(8,128)(2,1)S(1)} %get-tuple-element.73), channel_id=1, source_target_pairs={{8,0},{16,8},{24,16},{9,1},{17,9},{25,17},{10,2},{18,10},{26,18},{... | collective-permute-start | bytes 147464 | tf_op jit(solution)/shard_map/ppermute | solution.py:25
  65.8 5.4 %collective-permute-start.1 = (bf16[6,1,16,256]{3,2,1,0:T(8,128)(2,1)S(1)}, bf16[6,1,16,256]{3,2,1,0:T(8,128)(2,1)S(1)}, u32[]{:S(2)}, u32[]{:S(2)}) collective-permute-start(bf16[6,1,16,256]{3,2,1,0:T(8,128)(2,1)S(1)} %get-tuple-element.74), channel_id=1, source_target_pairs={{0,8},{8,16},{16,24},{1,9},{9,17},{17,25},{2,10},{10,18},{18,26},{... | collective-permute-start | bytes 147464 | tf_op jit(solution)/shard_map/ppermute | solution.py:23
  71.4 6.6 %collective-permute-start.4 = (bf16[6,18,1,256]{3,2,1,0:T(2,128)(2,1)S(1)}, bf16[6,18,1,256]{3,2,1,0:T(2,128)(2,1)S(1)}, u32[]{:S(2)}, u32[]{:S(2)}) collective-permute-start(bf16[6,18,1,256]{3,2,1,0:T(2,128)(2,1)S(1)} %get-tuple-element.48), channel_id=1, source_target_pairs={{1,0},{2,1},{3,2},{4,3},{5,4},{6,5},{7,6},{9,8},{10,9},{11,10},{12... | collective-permute-start | bytes 165896 | tf_op jit(solution)/shard_map/ppermute | solution.py:25
  73.3 8.8 %collective-permute-start.3 = (bf16[6,18,1,256]{3,2,1,0:T(2,128)(2,1)S(1)}, bf16[6,18,1,256]{3,2,1,0:T(2,128)(2,1)S(1)}, u32[]{:S(2)}, u32[]{:S(2)}) collective-permute-start(bf16[6,18,1,256]{3,2,1,0:T(2,128)(2,1)S(1)} %get-tuple-element.49), channel_id=1, source_target_pairs={{0,1},{1,2},{2,3},{3,4},{4,5},{5,6},{6,7},{8,9},{9,10},{10,11},{11... | collective-permute-start | bytes 165896 | tf_op jit(solution)/shard_map/ppermute | solution.py:23
  121.8 200.9 %all-gather.3.cloned.1.call-start = ((), (), s32[]{:S(2)}) async-start(), calls=%async_computation.2 | async-start | bytes 1990656 | tf_op jit(solution)/shard_map/all_gather | solution.py:91
  122.0 2.2 copy-start.1
  133.3 149.6 %copy-start.7 = (bf16[4,16,16,256]{3,2,1,0:T(8,128)(2,1)S(1)}, bf16[4,16,16,256]{3,2,1,0:T(8,128)(2,1)}, u32[]{:S(2)}) copy-start(bf16[4,16,16,256]{3,2,1,0:T(8,128)(2,1)} %get-tuple-element.35) | copy-start | bytes 1572868
  281.3 2.8 copy-start.10
  281.3 4.0 %copy-start.8 = (bf16[4,16,16,256]{3,2,1,0:T(8,128)(2,1)S(1)}, bf16[4,16,16,256]{3,2,1,0:T(8,128)(2,1)}, u32[]{:S(2)}) copy-start(bf16[4,16,16,256]{3,2,1,0:T(8,128)(2,1)} %get-tuple-element.26) | copy-start | bytes 1572868
  282.8 3.7 %copy-start.6 = (bf16[4,16,16,256]{3,2,1,0:T(8,128)(2,1)S(1)}, bf16[4,16,16,256]{3,2,1,0:T(8,128)(2,1)}, u32[]{:S(2)}) copy-start(bf16[4,16,16,256]{3,2,1,0:T(8,128)(2,1)} %get-tuple-element.34) | copy-start | bytes 1572868
  286.5 3.8 %copy-start.5 = (bf16[4,16,16,256]{3,2,1,0:T(8,128)(2,1)S(1)}, bf16[4,16,16,256]{3,2,1,0:T(8,128)(2,1)}, u32[]{:S(2)}) copy-start(bf16[4,16,16,256]{3,2,1,0:T(8,128)(2,1)} %get-tuple-element.33) | copy-start | bytes 1572868
  287.8 3.8 %copy-start.9 = (bf16[4,16,16,256]{3,2,1,0:T(8,128)(2,1)S(1)}, bf16[4,16,16,256]{3,2,1,0:T(8,128)(2,1)}, u32[]{:S(2)}) copy-start(bf16[4,16,16,256]{3,2,1,0:T(8,128)(2,1)} %get-tuple-element.56) | copy-start | bytes 1572868
  290.3 3.7 %copy-start.3 = (bf16[4,16,16,256]{3,2,1,0:T(8,128)(2,1)S(1)}, bf16[4,16,16,256]{3,2,1,0:T(8,128)(2,1)}, u32[]{:S(2)}) copy-start(bf16[4,16,16,256]{3,2,1,0:T(8,128)(2,1)} %param.4) | copy-start | bytes 1572868
Sparse Core Ops, SparseCore 0:
  121.9 157.6 reduce-scatter.1
  281.9 40.7 all-gather.2
